TPU v7x, 32 devices: a whole 2x2x4 slice. The times are simulated.
32 devices in a mesh: dom: 16 (over z, x, core), band: 2 (over y).
Axes of the slice: x: 2, y: 2, z: 4, core: 2. Of those that a mesh axis runs over, the one named last changes fastest.
Arguments:
- wavefun: float32 [13824, 512], P('dom', 'band')
- cell_ops: float32 [64, 343, 343], P('dom'), as said below
- cell_map: int32 [64, 343], P('dom'), may hold values from 0 to 1007, as said below
- face_list: int32 [2304], P('dom'), may hold values from 0 to 863, as said below
Outputs:
- ortho_bands: float32 [13824, 512], P('dom', 'band')
Inputs may be any that keep to these rules, and one draw needn't show every extreme that they name: `cell_map`: each row lists the 343 distinct local numbers of a cell's nodes; a number below 864 is a node of the cell's own domain, 864 + j stands for the j-th lower face node of the next domain (periodic over domains); every node of a domain belongs to some cell of that domain. `face_list`: the 144 entries of each domain are distinct node numbers of that domain. `cell_ops`: each cell's matrix is symmetric.
All inputs are finite; a program needn't handle non-finite values.
Results may differ from a plain program's by a relative error of at most 0.0001.
Values sent between devices are 32-bit elements; how exact they have to be, the bound alone decides.
A program may use at most 64 MiB of HBM per device.

v0:
```python
import jax
import jax.numpy as jnp
from jax import lax
from jax.sharding import PartitionSpec as P

DEGREE = 2
cheb_centre = 1.0
cheb_half = 1.6


def shifted(block, axis, distance):
    devices = range(lax.axis_size(axis))
    route = [((i - distance) % len(devices), i) for i in devices]
    return lax.ppermute(block, axis, route)


def on_device(wavefun, cell_ops, cell_map, face_list):
    owned_rows = wavefun.shape[0]
    block_width = wavefun.shape[1]
    flat_map = cell_map.reshape(-1)

    def local_apply(extended):
        cell_values = extended[flat_map].reshape(cell_map.shape[0], cell_map.shape[1], block_width)
        products = jnp.einsum(
            "cij,cjb->cib", cell_ops, cell_values, precision=lax.Precision.HIGHEST
        )
        return jnp.zeros_like(extended).at[flat_map].add(products.reshape(-1, block_width))

    def operate(vector):
        fetched = shifted(vector[face_list], "dom", -1)
        applied = local_apply(jnp.concatenate([vector, fetched], 0))
        returned = shifted(applied[owned_rows:], "dom", 1)
        return applied[:owned_rows].at[face_list].add(returned)

    latest = (operate(wavefun) - cheb_centre * wavefun) / cheb_half

    def advance(counter, carried):
        earlier, current = carried
        following = 2.0 * (operate(current) - cheb_centre * current) / cheb_half - earlier
        return (current, following)

    earlier, latest = lax.fori_loop(1, DEGREE, advance, (wavefun, latest))
    full_bands = lax.all_gather(latest, "band", axis=1, tiled=True)
    partial_value = jnp.einsum("nb,nc->bc", full_bands, full_bands, precision=lax.Precision.HIGHEST)
    margin = lax.psum(partial_value, "dom")
    norm_value = jnp.sqrt(jnp.sum(margin * margin) + 1e-06)
    full_width = margin.shape[0]
    offset = lax.axis_index("band") * block_width
    scaled_cols = lax.dynamic_slice_in_dim(margin, offset, block_width, 1) / norm_value
    identity_cols = lax.dynamic_slice_in_dim(
        jnp.eye(full_width, dtype=jnp.float32), offset, block_width, 1
    )
    mixing = (3.0 * identity_cols - scaled_cols) / 2.0
    return jnp.dot(full_bands, mixing, precision=lax.Precision.HIGHEST)


def solution(mesh):
    return jax.shard_map(
        on_device,
        mesh=mesh,
        in_specs=(P("dom", "band"), P("dom", None, None), P("dom", None), P("dom")),
        out_specs=P("dom", "band"),
        check_vma=False,
    )
```

profile of v0, /device:TPU:0, one launch (start us, length us, event | category | flops | bytes accessed | tf_op | source)
XLA Modules:
  0.0 234.2 jit_solution(618638592340945098)
XLA Ops:
  6.5 0.8 compare_select_fusion.1
  7.4 2.0 gather_fusion
  9.3 5.5 %collective-permute-start = (f32[144,256]{1,0:T(8,128)S(1)}, f32[144,256]{1,0:T(8,128)S(1)}, u32[]{:S(2)}, u32[]{:S(2)}) collective-permute-start(f32[144,256]{1,0:T(8,128)S(1)} %gather_fusion), channel_id=1, source_target_pairs={{2,0},{4,2},{6,4},{8,6},{10,8},{12,10},{14,12},{16,14},{18,16},{20... | collective-permute-start | bytes 442376 | tf_op jit(solution)/shard_map/ppermute | solution.py:14
  15.7 1.9 collective-permute-done
  17.5 1.2 pad_maximum_fusion
  18.7 4.6 %gather_fusion.1 = f32[1372,256]{1,0:T(8,128)} fusion(f32[1008,256]{1,0:T(8,128)S(1)} %pad_maximum_fusion, s32[2048]{0:T(1024)S(1)} %pad_clamp_fusion), kind=kCustom, calls=%fused_computation.1 | custom fusion | bytes 2815344 | tf_op jit(solution)/shard_map/gather | solution.py:23
  23.3 1.5 reshape.46
  24.8 3.7 %fusion.4 = f32[4,343,256]{2,1,0:T(8,128)} fusion(f32[4,343,256]{2,1,0:T(8,128)S(1)} %reshape.46, f32[4,343,343]{2,0,1:T(4,128)S(1)} %copy-done), kind=kOutput, calls=%fused_computation.12 | convolution fusion | flops 1445670912 | bytes 4692240 | tf_op jit(solution)/shard_map/cij,cjb->cib/dot_general | solution.py:24
  28.5 2.6 %reshape.86 = f32[1372,256]{1,0:T(8,128)} reshape(f32[4,343,256]{2,1,0:T(8,128)} %fusion.4) | data formatting | bytes 2809856 | tf_op jit(solution)/shard_map/reshape | solution.py:27
  31.1 8.7 %scatter_custom_fusion = f32[1008,256]{1,0:T(8,128)S(1)} fusion(s32[1372]{0:T(1024)S(1)} %fusion.25, f32[1372,256]{1,0:T(8,128)} %reshape.86, f32[]{:T(128)} %constant.12.clone.1), kind=kCustom, calls=%fused_computation.29 | custom fusion | flops 351232 | bytes 1032704 | tf_op jit(solution)/shard_map/scatter-add | solution.py:27
  39.9 1.0 copy-done.3
  40.9 1.2 slice.26
  42.1 6.2 %collective-permute-done.1 = f32[144,256]{1,0:T(8,128)S(1)} collective-permute-done((f32[144,256]{1,0:T(8,128)S(1)}, f32[144,256]{1,0:T(8,128)S(1)}, u32[]{:S(2)}, u32[]{:S(2)}) %collective-permute-start.1) | collective-permute-done | bytes 147488 | tf_op jit(solution)/shard_map/ppermute | solution.py:14
  48.3 1.7 scatter_fusion
  50.0 2.6 %subtract_multiply_fusion = f32[864,256]{1,0:T(8,128)} fusion(f32[864,256]{1,0:T(8,128)S(1)} %scatter_fusion, f32[864,256]{1,0:T(8,128)} %param.4), kind=kLoop, calls=%fused_computation.18 | loop fusion | flops 442368 | bytes 2654208 | tf_op jit(solution)/shard_map/div | solution.py:35
  52.5 2.0 gather_fusion.2
  54.8 2.7 %collective-permute-done.2 = f32[144,256]{1,0:T(8,128)S(1)} collective-permute-done((f32[144,256]{1,0:T(8,128)S(1)}, f32[144,256]{1,0:T(8,128)S(1)}, u32[]{:S(2)}, u32[]{:S(2)}) %collective-permute-start.2) | collective-permute-done | bytes 147488 | tf_op jit(solution)/shard_map/while/body/eval_jaxpr/ppermute | solution.py:14
  57.4 1.2 pad_maximum_fusion.1
  58.7 4.6 %gather_fusion.3 = f32[1372,256]{1,0:T(8,128)} fusion(f32[1008,256]{1,0:T(8,128)S(1)} %pad_maximum_fusion.1, s32[2048]{0:T(1024)S(1)} %pad_clamp_fusion), kind=kCustom, calls=%fused_computation.3 | custom fusion | bytes 2815344 | tf_op jit(solution)/shard_map/while/body/eval_jaxpr/gather | solution.py:23
  63.2 1.5 reshape.48
  64.7 3.7 %fusion.7 = f32[4,343,256]{2,1,0:T(8,128)} fusion(f32[4,343,256]{2,1,0:T(8,128)S(1)} %reshape.48, f32[4,343,343]{2,0,1:T(4,128)S(1)} %copy-done), kind=kOutput, calls=%fused_computation.13 | convolution fusion | flops 1445670912 | bytes 4692240 | tf_op jit(solution)/shard_map/while/body/eval_jaxpr/cij,cjb->cib/dot_general | solution.py:24
  68.4 2.6 %reshape.102 = f32[1372,256]{1,0:T(8,128)} reshape(f32[4,343,256]{2,1,0:T(8,128)} %fusion.7) | data formatting | bytes 2809856 | tf_op jit(solution)/shard_map/while/body/eval_jaxpr/reshape | solution.py:27
  71.0 8.7 %scatter_custom_fusion.2 = f32[1008,256]{1,0:T(8,128)S(1)} fusion(s32[1372]{0:T(1024)S(1)} %fusion.25, f32[1372,256]{1,0:T(8,128)} %reshape.102, f32[]{:T(128)} %constant.12.clone.1), kind=kCustom, calls=%fused_computation.27 | custom fusion | flops 351232 | bytes 1032704 | tf_op jit(solution)/shard_map/while/body/eval_jaxpr/scatter-add | solution.py:27
  79.8 1.0 slice.28
  80.8 6.4 %collective-permute-done.3 = f32[144,256]{1,0:T(8,128)S(1)} collective-permute-done((f32[144,256]{1,0:T(8,128)S(1)}, f32[144,256]{1,0:T(8,128)S(1)}, u32[]{:S(2)}, u32[]{:S(2)}) %collective-permute-start.3) | collective-permute-done | bytes 147488 | tf_op jit(solution)/shard_map/while/body/eval_jaxpr/ppermute | solution.py:14
  87.3 3.3 %scatter_fusion.1 = f32[864,256]{1,0:T(8,128)} fusion(f32[864,256]{1,0:T(8,128)} %slice.28, s32[144]{0:T(256)S(1)} %compare_select_fusion.1, f32[144,256]{1,0:T(8,128)S(1)} %collective-permute-done.3), kind=kCustom, calls=%fused_computation.7 | custom fusion | flops 36864 | bytes 442944 | tf_op jit(solution)/shard_map/while/body/eval_jaxpr/scatter-add | solution.py:33
  90.6 2.6 %multiply_subtract_fusion = f32[864,256]{1,0:T(8,128)} fusion(f32[864,256]{1,0:T(8,128)} %param.4, f32[864,256]{1,0:T(8,128)} %scatter_fusion.1, f32[864,256]{1,0:T(8,128)S(1)} %copy-done.2), kind=kLoop, calls=%fused_computation.17 | loop fusion | flops 1105920 | bytes 3538944 | tf_op jit(solution)/shard_map/while/body/eval_jaxpr/sub | solution.py:39
  93.5 26.6 %all-gather.2.cloned.1.call-done = f32[864,512]{1,0:T(8,128)} async-done(((f32[864,256]{1,0:T(8,128)}), f32[864,512]{1,0:T(8,128)}) %all-gather.2.cloned.1.call-update) | async-done | bytes 1769488 | tf_op jit(solution)/shard_map/all_gather | solution.py:43
  120.0 6.5 %fusion.29 = f32[512,512]{1,0:T(8,128)} fusion(f32[864,512]{1,0:T(8,128)} %all-gather.2.cloned.1.call-done), kind=kOutput, calls=%fused_computation.43 | convolution fusion | flops 2717908992 | bytes 2818048 | tf_op jit(solution)/shard_map/nb,nc->bc/dot_general | solution.py:44
  126.6 93.8 %all-reduce.2.cloned.1.call-done = f32[512,512]{1,0:T(8,128)} async-done(((f32[512,512]{1,0:T(8,128)}), f32[512,512]{1,0:T(8,128)}) %all-reduce.2.cloned.1.call-update) | async-done | bytes 1048592 | tf_op jit(solution)/shard_map/psum | solution.py:45
  220.5 2.1 multiply_reduce_fusion
  223.2 4.1 %fusion.10 = f32[864,256]{1,0:T(8,128)} fusion(f32[864,512]{1,0:T(8,128)} %all-gather.2.cloned.1.call-done, f32[512,512]{1,0:T(8,128)} %all-reduce.2.cloned.1.call-done, s32[]{:T(128)S(6)} %select_n.27, f32[]{:T(128)S(6)} %sqrt.3), kind=kOutput, calls=%fused_computation.20 | convolution fusion | flops 1359872000 | bytes 3180032 | tf_op jit(solution)/shard_map/dot_general | solution.py:54
  (20 shorter events, 1.4 us)
Async XLA Ops:
  6.5 18.3 %copy-start = (f32[4,343,343]{2,0,1:T(4,128)S(1)}, f32[4,343,343]{2,0,1:T(4,128)}, u32[]{:S(2)}) copy-start(f32[4,343,343]{2,0,1:T(4,128)} %param.5) | copy-start | bytes 5647156
  6.5 113.5 %all-gather.2.cloned.1.call-start = ((), (), s32[]{:S(2)}) async-start(), calls=%async_computation | async-start | bytes 2654208 | tf_op jit(solution)/shard_map/all_gather | solution.py:43
  9.3 8.2 %collective-permute-start = (f32[144,256]{1,0:T(8,128)S(1)}, f32[144,256]{1,0:T(8,128)S(1)}, u32[]{:S(2)}, u32[]{:S(2)}) collective-permute-start(f32[144,256]{1,0:T(8,128)S(1)} %gather_fusion), channel_id=1, source_target_pairs={{2,0},{4,2},{6,4},{8,6},{10,8},{12,10},{14,12},{16,14},{18,16},{20... | collective-permute-start | bytes 442376 | tf_op jit(solution)/shard_map/ppermute | solution.py:14
  39.9 1.0 copy-start.3
  40.8 7.4 %collective-permute-start.1 = (f32[144,256]{1,0:T(8,128)S(1)}, f32[144,256]{1,0:T(8,128)S(1)}, u32[]{:S(2)}, u32[]{:S(2)}) collective-permute-start(f32[144,256]{1,0:T(8,128)S(1)} %slice.27), channel_id=1, source_target_pairs={{30,0},{0,2},{2,4},{4,6},{6,8},{8,10},{10,12},{12,14},{14,16},{16,... | collective-permute-start | bytes 442376 | tf_op jit(solution)/shard_map/ppermute | solution.py:14
  50.0 4.5 %copy-start.1 = (f32[864,256]{1,0:T(8,128)}, f32[864,256]{1,0:T(8,128)S(1)}, u32[]{:S(2)}) copy-start(f32[864,256]{1,0:T(8,128)S(1)} %scatter_fusion) | copy-start | bytes 2654212
  54.5 2.9 %collective-permute-start.2 = (f32[144,256]{1,0:T(8,128)S(1)}, f32[144,256]{1,0:T(8,128)S(1)}, u32[]{:S(2)}, u32[]{:S(2)}) collective-permute-start(f32[144,256]{1,0:T(8,128)S(1)} %gather_fusion.2), channel_id=1, source_target_pairs={{2,0},{4,2},{6,4},{8,6},{10,8},{12,10},{14,12},{16,14},{18,16},{20... | collective-permute-start | bytes 442376 | tf_op jit(solution)/shard_map/while/body/eval_jaxpr/ppermute | solution.py:14
  79.8 7.5 %collective-permute-start.3 = (f32[144,256]{1,0:T(8,128)S(1)}, f32[144,256]{1,0:T(8,128)S(1)}, u32[]{:S(2)}, u32[]{:S(2)}) collective-permute-start(f32[144,256]{1,0:T(8,128)S(1)} %slice.29), channel_id=1, source_target_pairs={{30,0},{0,2},{2,4},{4,6},{6,8},{8,10},{10,12},{12,14},{14,16},{16,... | collective-permute-start | bytes 442376 | tf_op jit(solution)/shard_map/while/body/eval_jaxpr/ppermute | solution.py:14
  80.8 9.8 %copy-start.2 = (f32[864,256]{1,0:T(8,128)S(1)}, f32[864,256]{1,0:T(8,128)}, u32[]{:S(2)}) copy-start(f32[864,256]{1,0:T(8,128)} %copy-done.1) | copy-start | bytes 2654212
  93.2 127.3 %all-reduce.2.cloned.1.call-start = ((), (), s32[]{:S(2)}) async-start(), calls=%async_computation.1 | async-start | bytes 2097152 | tf_op jit(solution)/shard_map/psum | solution.py:45
Sparse Core Ops, SparseCore 0:
  93.3 26.6 all-gather.1
  126.7 93.6 all-reduce.1
where the time goes:
time: 235 us; the launch traced here: 234 us
  waiting for transfers between devices  138 us (59%)
  other arithmetic  33.1 us (14%)
  local copies, waits for them, and re-layouts  25.3 us (11%)
  matrix products  18 us (8%)
  between operations  14.2 us (6%)
  starting transfers between devices  6.06 us (3%)
    psum x1, waiting for transfers between devices, on_device(): margin = lax.psum(partial_value, 'dom')  93.8 us
    all_gather x1, waiting for transfers between devices, on_device(): full_bands = lax.all_gather(latest, 'band', axis=1, tiled=True)  26.6 us
    scatter-add x2, other arithmetic, local_apply(): jnp.zeros_like(extended).at[flat_map].add(products.reshape(-1, block_width))  17.4 us
    ppermute x4, waiting for transfers between devices, shifted(): return lax.ppermute(block, axis, route)  17.1 us
    gather x2, local copies, waits for them, and re-layouts, local_apply(): extended[flat_map]  9.14 us
    dot_general x2, matrix products, local_apply(): jnp.einsum('cij,cjb->cib', cell_ops, cell_values, precision=lax.Precision...  7.36 us
    dot_general x1, matrix products, on_device(): jnp.einsum('nb,nc->bc', full_bands, full_bands, precision=lax.Precision.H...  6.54 us
    ppermute x4, starting transfers between devices, shifted(): return lax.ppermute(block, axis, route)  5.8 us
  transfers between devices with their start and end apart: 6, of which 6 were waited for; matrix products, arithmetic and copies ran while one was open for 1% of the time, Pallas kernels for 0%

commit v1 on v0

--- a/solution.py
+++ b/solution.py
@@ -6,6 +6,29 @@
 DEGREE = 2
 cheb_centre = 1.0
 cheb_half = 1.6
+
+
+def spans_pass(mine):
+    dev_axis = "band"
+    inter = lax.axis_size(dev_axis)
+    moved = lax.axis_index(dev_axis)
+    low, mid_arr, work_now = (inter, moved, mine.shape[1])
+    last, current_value = (mine, 1)
+    while current_value < low:
+        last = jnp.concatenate(
+            [
+                last,
+                lax.ppermute(
+                    last,
+                    axis_name=dev_axis,
+                    perm=[(dev_j, (dev_j - current_value) % low) for dev_j in range(low)],
+                ),
+            ],
+            1,
+        )
+        current_value = 2 * current_value
+    d_next = jnp.roll(last, mid_arr * work_now, 1)
+    return d_next
 
 
 def shifted(block, axis, distance):
@@ -40,7 +63,7 @@
         return (current, following)
 
     earlier, latest = lax.fori_loop(1, DEGREE, advance, (wavefun, latest))
-    full_bands = lax.all_gather(latest, "band", axis=1, tiled=True)
+    full_bands = spans_pass(latest)
     partial_value = jnp.einsum("nb,nc->bc", full_bands, full_bands, precision=lax.Precision.HIGHEST)
     margin = lax.psum(partial_value, "dom")
     norm_value = jnp.sqrt(jnp.sum(margin * margin) + 1e-06)

time: 235 us -> 227 us (0.966)
  waiting for transfers between devices: 138 us -> 128 us
    all_gather x1 -> x0, waiting for transfers between devices: 26.6 us -> none  [on_device(): full_bands = lax.all_gather(latest, 'band', axis=1, tiled=True)]
    ppermute x0 -> x1, waiting for transfers between devices: none -> 14.2 us  [spans_pass(): lax.ppermute(last, axis_name=dev_axis, perm=[(dev_j, (dev_j - current_val...]
    psum x1, waiting for transfers between devices: 93.8 us -> 96.2 us  [on_device(): margin = lax.psum(partial_value, 'dom')]
where the time goes in v1:
time: 227 us; the launch traced here: 226 us
  waiting for transfers between devices  128 us (56%)
  other arithmetic  34.6 us (15%)
  local copies, waits for them, and re-layouts  26.5 us (12%)
  matrix products  16 us (7%)
  between operations  14.2 us (6%)
  starting transfers between devices  7.32 us (3%)
    psum x1, waiting for transfers between devices, on_device(): margin = lax.psum(partial_value, 'dom')  96.2 us
    scatter-add x2, other arithmetic, local_apply(): jnp.zeros_like(extended).at[flat_map].add(products.reshape(-1, block_width))  17.4 us
    ppermute x4, waiting for transfers between devices, shifted(): return lax.ppermute(block, axis, route)  17.1 us
    ppermute x1, waiting for transfers between devices, spans_pass(): lax.ppermute(last, axis_name=dev_axis, perm=[(dev_j, (dev_j - current_val...  14.2 us
    gather x2, local copies, waits for them, and re-layouts, local_apply(): extended[flat_map]  9.14 us
    dot_general x2, matrix products, local_apply(): jnp.einsum('cij,cjb->cib', cell_ops, cell_values, precision=lax.Precision...  7.36 us
    ppermute x4, starting transfers between devices, shifted(): return lax.ppermute(block, axis, route)  5.8 us
    reshape x2, local copies, waits for them, and re-layouts, local_apply(): products.reshape(-1, block_width)  5.23 us
  transfers between devices with their start and end apart: 6, of which 6 were waited for; matrix products, arithmetic and copies ran while one was open for 1% of the time, Pallas kernels for 0%

profile of v1, /device:TPU:0, one launch (start us, length us, event | category | flops | bytes accessed | tf_op | source)
XLA Modules:
  0.0 226.2 jit_solution(11402799181223061827)
XLA Ops:
  7.4 2.0 gather_fusion
  9.3 5.5 %collective-permute-start = (f32[144,256]{1,0:T(8,128)S(1)}, f32[144,256]{1,0:T(8,128)S(1)}, u32[]{:S(2)}, u32[]{:S(2)}) collective-permute-start(f32[144,256]{1,0:T(8,128)S(1)} %gather_fusion), channel_id=1, source_target_pairs={{2,0},{4,2},{6,4},{8,6},{10,8},{12,10},{14,12},{16,14},{18,16},{20... | collective-permute-start | bytes 442376 | tf_op jit(solution)/shard_map/ppermute | solution.py:37
  15.7 1.9 collective-permute-done
  17.5 1.2 pad_maximum_fusion
  18.7 4.6 %gather_fusion.1 = f32[1372,256]{1,0:T(8,128)} fusion(f32[1008,256]{1,0:T(8,128)S(1)} %pad_maximum_fusion, s32[2048]{0:T(1024)S(1)} %pad_clamp_fusion), kind=kCustom, calls=%fused_computation.1 | custom fusion | bytes 2815344 | tf_op jit(solution)/shard_map/gather | solution.py:46
  23.3 1.5 reshape.46
  24.8 3.7 %fusion.7 = f32[4,343,256]{2,1,0:T(8,128)} fusion(f32[4,343,256]{2,1,0:T(8,128)S(1)} %reshape.46, f32[4,343,343]{2,0,1:T(4,128)S(1)} %copy-done), kind=kOutput, calls=%fused_computation.19 | convolution fusion | flops 1445670912 | bytes 4692240 | tf_op jit(solution)/shard_map/cij,cjb->cib/dot_general | solution.py:47
  28.5 2.6 %reshape.86 = f32[1372,256]{1,0:T(8,128)} reshape(f32[4,343,256]{2,1,0:T(8,128)} %fusion.7) | data formatting | bytes 2809856 | tf_op jit(solution)/shard_map/reshape | solution.py:50
  31.1 8.7 %scatter_custom_fusion = f32[1008,256]{1,0:T(8,128)S(1)} fusion(s32[1372]{0:T(1024)S(1)} %fusion.28, f32[1372,256]{1,0:T(8,128)} %reshape.86, f32[]{:T(128)} %constant.34.clone.1), kind=kCustom, calls=%fused_computation.36 | custom fusion | flops 351232 | bytes 1032704 | tf_op jit(solution)/shard_map/scatter-add | solution.py:50
  40.9 1.2 slice.26
  42.1 6.2 %collective-permute-done.1 = f32[144,256]{1,0:T(8,128)S(1)} collective-permute-done((f32[144,256]{1,0:T(8,128)S(1)}, f32[144,256]{1,0:T(8,128)S(1)}, u32[]{:S(2)}, u32[]{:S(2)}) %collective-permute-start.1) | collective-permute-done | bytes 147488 | tf_op jit(solution)/shard_map/ppermute | solution.py:37
  48.3 1.7 scatter_fusion
  50.0 2.6 %subtract_multiply_fusion = f32[864,256]{1,0:T(8,128)} fusion(f32[864,256]{1,0:T(8,128)S(1)} %scatter_fusion, f32[864,256]{1,0:T(8,128)} %param.4), kind=kLoop, calls=%fused_computation.25 | loop fusion | flops 442368 | bytes 2654208 | tf_op jit(solution)/shard_map/div | solution.py:58
  52.5 2.0 gather_fusion.2
  54.8 2.7 %collective-permute-done.2 = f32[144,256]{1,0:T(8,128)S(1)} collective-permute-done((f32[144,256]{1,0:T(8,128)S(1)}, f32[144,256]{1,0:T(8,128)S(1)}, u32[]{:S(2)}, u32[]{:S(2)}) %collective-permute-start.2) | collective-permute-done | bytes 147488 | tf_op jit(solution)/shard_map/while/body/eval_jaxpr/ppermute | solution.py:37
  57.4 1.2 pad_maximum_fusion.1
  58.7 4.6 %gather_fusion.3 = f32[1372,256]{1,0:T(8,128)} fusion(f32[1008,256]{1,0:T(8,128)S(1)} %pad_maximum_fusion.1, s32[2048]{0:T(1024)S(1)} %pad_clamp_fusion), kind=kCustom, calls=%fused_computation.3 | custom fusion | bytes 2815344 | tf_op jit(solution)/shard_map/while/body/eval_jaxpr/gather | solution.py:46
  63.2 1.5 reshape.48
  64.7 3.7 %fusion.10 = f32[4,343,256]{2,1,0:T(8,128)} fusion(f32[4,343,256]{2,1,0:T(8,128)S(1)} %reshape.48, f32[4,343,343]{2,0,1:T(4,128)S(1)} %copy-done), kind=kOutput, calls=%fused_computation.20 | convolution fusion | flops 1445670912 | bytes 4692240 | tf_op jit(solution)/shard_map/while/body/eval_jaxpr/cij,cjb->cib/dot_general | solution.py:47
  68.4 2.6 %reshape.102 = f32[1372,256]{1,0:T(8,128)} reshape(f32[4,343,256]{2,1,0:T(8,128)} %fusion.10) | data formatting | bytes 2809856 | tf_op jit(solution)/shard_map/while/body/eval_jaxpr/reshape | solution.py:50
  71.0 8.7 %scatter_custom_fusion.2 = f32[1008,256]{1,0:T(8,128)S(1)} fusion(s32[1372]{0:T(1024)S(1)} %fusion.28, f32[1372,256]{1,0:T(8,128)} %reshape.102, f32[]{:T(128)} %constant.34.clone.1), kind=kCustom, calls=%fused_computation.34 | custom fusion | flops 351232 | bytes 1032704 | tf_op jit(solution)/shard_map/while/body/eval_jaxpr/scatter-add | solution.py:50
  80.8 6.4 %collective-permute-done.3 = f32[144,256]{1,0:T(8,128)S(1)} collective-permute-done((f32[144,256]{1,0:T(8,128)S(1)}, f32[144,256]{1,0:T(8,128)S(1)}, u32[]{:S(2)}, u32[]{:S(2)}) %collective-permute-start.3) | collective-permute-done | bytes 147488 | tf_op jit(solution)/shard_map/while/body/eval_jaxpr/ppermute | solution.py:37
  87.3 3.3 %scatter_fusion.1 = f32[864,256]{1,0:T(8,128)} fusion(f32[864,256]{1,0:T(8,128)} %slice.28, s32[144]{0:T(256)S(1)} %compare_select_fusion.1, f32[144,256]{1,0:T(8,128)S(1)} %collective-permute-done.3), kind=kCustom, calls=%fused_computation.7 | custom fusion | flops 36864 | bytes 442944 | tf_op jit(solution)/shard_map/while/body/eval_jaxpr/scatter-add | solution.py:56
  90.6 2.6 %multiply_subtract_fusion = f32[864,256]{1,0:T(8,128)} fusion(f32[864,256]{1,0:T(8,128)} %param.4, f32[864,256]{1,0:T(8,128)} %scatter_fusion.1, f32[864,256]{1,0:T(8,128)S(1)} %copy-done.3), kind=kLoop, calls=%fused_computation.24 | loop fusion | flops 1105920 | bytes 3538944 | tf_op jit(solution)/shard_map/while/body/eval_jaxpr/sub | solution.py:62
  93.2 1.5 collective-permute-start.4
  94.7 14.2 %collective-permute-done.4 = f32[864,256]{1,0:T(8,128)S(1)} collective-permute-done((f32[864,256]{1,0:T(8,128)}, f32[864,256]{1,0:T(8,128)S(1)}, u32[]{:S(2)}, u32[]{:S(2)}) %collective-permute-start.4) | collective-permute-done | bytes 884768 | tf_op jit(solution)/shard_map/ppermute | solution.py:21
  108.9 1.6 fusion.6
  110.5 1.2 copy-done.1
  111.7 4.5 %fusion.32 = f32[512,512]{1,0:T(8,128)} fusion(f32[864,512]{1,0:T(8,128)S(1)} %fusion.6), kind=kOutput, calls=%fused_computation.50 | convolution fusion | flops 2717908992 | bytes 2818048 | tf_op jit(solution)/shard_map/nb,nc->bc/dot_general | solution.py:67
  116.2 96.2 %all-reduce.2.cloned.1.call-done = f32[512,512]{1,0:T(8,128)} async-done(((f32[512,512]{1,0:T(8,128)}), f32[512,512]{1,0:T(8,128)}) %all-reduce.2.cloned.1.call-update) | async-done | bytes 1048592 | tf_op jit(solution)/shard_map/psum | solution.py:68
  212.4 2.1 multiply_reduce_fusion
  215.2 4.1 %fusion.13 = f32[864,256]{1,0:T(8,128)} fusion(f32[864,512]{1,0:T(8,128)} %copy-done.1, f32[512,512]{1,0:T(8,128)} %all-reduce.2.cloned.1.call-done, s32[]{:T(128)S(6)} %select_n.42, f32[]{:T(128)S(6)} %sqrt.3), kind=kOutput, calls=%fused_computation.27 | convolution fusion | flops 1359872000 | bytes 3180032 | tf_op jit(solution)/shard_map/dot_general | solution.py:77
  (22 shorter events, 3.9 us)
Async XLA Ops:
  6.5 18.3 %copy-start = (f32[4,343,343]{2,0,1:T(4,128)S(1)}, f32[4,343,343]{2,0,1:T(4,128)}, u32[]{:S(2)}) copy-start(f32[4,343,343]{2,0,1:T(4,128)} %param.5) | copy-start | bytes 5647156
  6.5 205.9 %all-reduce.2.cloned.1.call-start = ((), (), s32[]{:S(2)}) async-start(), calls=%async_computation | async-start | bytes 2097152 | tf_op jit(solution)/shard_map/psum | solution.py:68
  9.3 8.2 %collective-permute-start = (f32[144,256]{1,0:T(8,128)S(1)}, f32[144,256]{1,0:T(8,128)S(1)}, u32[]{:S(2)}, u32[]{:S(2)}) collective-permute-start(f32[144,256]{1,0:T(8,128)S(1)} %gather_fusion), channel_id=1, source_target_pairs={{2,0},{4,2},{6,4},{8,6},{10,8},{12,10},{14,12},{16,14},{18,16},{20... | collective-permute-start | bytes 442376 | tf_op jit(solution)/shard_map/ppermute | solution.py:37
  39.9 1.0 copy-start.4
  40.8 7.4 %collective-permute-start.1 = (f32[144,256]{1,0:T(8,128)S(1)}, f32[144,256]{1,0:T(8,128)S(1)}, u32[]{:S(2)}, u32[]{:S(2)}) collective-permute-start(f32[144,256]{1,0:T(8,128)S(1)} %slice.27), channel_id=1, source_target_pairs={{30,0},{0,2},{2,4},{4,6},{6,8},{8,10},{10,12},{12,14},{14,16},{16,... | collective-permute-start | bytes 442376 | tf_op jit(solution)/shard_map/ppermute | solution.py:37
  50.0 4.5 %copy-start.2 = (f32[864,256]{1,0:T(8,128)}, f32[864,256]{1,0:T(8,128)S(1)}, u32[]{:S(2)}) copy-start(f32[864,256]{1,0:T(8,128)S(1)} %scatter_fusion) | copy-start | bytes 2654212
  54.5 2.9 %collective-permute-start.2 = (f32[144,256]{1,0:T(8,128)S(1)}, f32[144,256]{1,0:T(8,128)S(1)}, u32[]{:S(2)}, u32[]{:S(2)}) collective-permute-start(f32[144,256]{1,0:T(8,128)S(1)} %gather_fusion.2), channel_id=1, source_target_pairs={{2,0},{4,2},{6,4},{8,6},{10,8},{12,10},{14,12},{16,14},{18,16},{20... | collective-permute-start | bytes 442376 | tf_op jit(solution)/shard_map/while/body/eval_jaxpr/ppermute | solution.py:37
  79.8 7.5 %collective-permute-start.3 = (f32[144,256]{1,0:T(8,128)S(1)}, f32[144,256]{1,0:T(8,128)S(1)}, u32[]{:S(2)}, u32[]{:S(2)}) collective-permute-start(f32[144,256]{1,0:T(8,128)S(1)} %slice.29), channel_id=1, source_target_pairs={{30,0},{0,2},{2,4},{4,6},{6,8},{8,10},{10,12},{12,14},{14,16},{16,... | collective-permute-start | bytes 442376 | tf_op jit(solution)/shard_map/while/body/eval_jaxpr/ppermute | solution.py:37
  80.8 9.8 %copy-start.3 = (f32[864,256]{1,0:T(8,128)S(1)}, f32[864,256]{1,0:T(8,128)}, u32[]{:S(2)}) copy-start(f32[864,256]{1,0:T(8,128)} %copy-done.2) | copy-start | bytes 2654212
  93.2 15.7 %collective-permute-start.4 = (f32[864,256]{1,0:T(8,128)}, f32[864,256]{1,0:T(8,128)S(1)}, u32[]{:S(2)}, u32[]{:S(2)}) collective-permute-start(f32[864,256]{1,0:T(8,128)} %multiply_subtract_fusion), channel_id=1, source_target_pairs={{0,1},{1,0},{2,3},{3,2},{4,5},{5,4},{6,7},{7,6},{8,9},{9,8},{10,11... | collective-permute-start | bytes 2654216 | tf_op jit(solution)/shard_map/ppermute | solution.py:21
  110.5 1.2 copy-start.1
Sparse Core Ops, SparseCore 0:
  116.3 96.0 all-reduce.1
